TPU v7x, 512 devices: a whole 4x4x16 slice. The times are simulated.
512 devices in a mesh: pb: 16 (over y_hi, x, core), lab: 32 (over y_lo, z).
Axes of the slice: x: 4, y: 4 (y_hi: 2, y_lo: 2; y = y_hi * 2 + y_lo), z: 16, core: 2. Of those that a mesh axis runs over, the one named last changes fastest.
Arguments:
- queries: bfloat16 [16384, 768], P(('pb', 'lab')), may hold values from -6 to 6
- label_weights: bfloat16 [32768, 768], P('lab'), may hold values from -0.21875 to 0.21875
- sibling_blocks: int32 [16384, 8], P('pb'), may hold values from 0 to 255, as said below
- positive_slot: int32 [16384], P('pb'), may hold values from 0 to 1023
Outputs:
- query_grad: float32 [16384, 768], P(('pb', 'lab'))
- weight_grad: bfloat16 [32768, 768], P('lab')
Inputs may be any that keep to these rules, and one draw needn't show every extreme that they name: `sibling_blocks`: each row names 8 different cluster blocks, lying in 8 different runs of 8 blocks (block // 8 differs). Rows are taken in aligned runs of 32 (one device's queries): within each run, exactly 8 rows name a block of each run of 8 blocks. Within each query group (aligned blocks of 1024 rows) no block is named by more than 144 rows, and some block is named by exactly 144 rows.
All inputs are finite; a program needn't handle non-finite values.
Results may differ from a plain program's by a relative error of at most 0.0047.
Values may be sent and summed in bfloat16 or wider, within the bound.
A program may use at most 64 MiB of HBM per device.

v0:
```python
import jax
import jax.numpy as jnp
from jax import lax
from jax.sharding import PartitionSpec as P

BLOCK = 128


def shards(queries, label_weights, sibling_blocks, positive_slot):
    lab_dev = label_weights.shape[0]
    blocks_dev = lab_dev // BLOCK
    first = lax.axis_index("lab") * blocks_dev
    local_ids = first + jnp.arange(blocks_dev, dtype=jnp.int32)
    pblock = jnp.take_along_axis(sibling_blocks, (positive_slot // BLOCK)[:, None], axis=1)[:, 0]
    positive = pblock * BLOCK + positive_slot % BLOCK
    label_ids = local_ids[:, None] * BLOCK + jnp.arange(BLOCK, dtype=jnp.int32)[None, :]
    chosen_all = jnp.any(sibling_blocks[:, :, None] == local_ids[None, None, :], axis=1)
    piece = lax.all_gather(queries, "lab", axis=0, tiled=True)
    count = piece.shape[0]
    scores = jnp.dot(piece, label_weights.T, preferred_element_type=jnp.float32)
    scores = scores.reshape(count, blocks_dev, BLOCK)
    target = (label_ids[None, :, :] == positive[:, None, None]).astype(jnp.float32)
    slope = jnp.where(chosen_all[:, :, None], jax.nn.sigmoid(scores) - target, 0.0)
    slope = slope.astype(jnp.bfloat16).reshape(count, lab_dev)
    dq_rows = jnp.dot(slope, label_weights, preferred_element_type=jnp.float32)
    dq_all = dq_rows
    w_acc = lax.dot_general(
        slope, piece, (((0,), (0,)), ((), ())), preferred_element_type=jnp.float32
    )
    dq_all, w_acc = (dq_all, w_acc)
    query_grad = lax.psum_scatter(dq_all, "lab", scatter_dimension=0, tiled=True)
    groups = lax.axis_size("pb")
    total = lax.psum(w_acc, "pb")
    weight_grad = (total / groups).astype(jnp.bfloat16)
    return (query_grad, weight_grad)


def solution(mesh):
    in_specs = (P(("pb", "lab"), None), P("lab", None), P("pb", None), P("pb"))
    out_specs = (P(("pb", "lab"), None), P("lab", None))
    return jax.shard_map(shards, mesh=mesh, in_specs=in_specs, out_specs=out_specs, check_vma=False)
```

profile of v0, /device:TPU:6, one launch (start us, length us, event | category | flops | bytes accessed | tf_op | source)
XLA Modules:
  0.0 469.2 jit_solution(15518499870351268009)
XLA Ops:
  7.2 0.0 copy-start
  7.2 0.0 copy-start.1
  7.2 0.0 all-gather.2.cloned.1.call-start
  7.2 0.7 all-gather.2.cloned.1.call-update
  7.9 0.0 all-reduce.2.cloned.1.call-start
  8.0 0.9 compare_reduce_fusion
  8.9 0.3 copy.8
  9.1 0.7 compare_select_fusion
  9.9 0.0 copy-done.1
  9.9 0.0 copy-start.2
  9.9 6.5 %gather_fusion = s32[1024]{0:T(1024)S(1)} fusion(s32[1024,8]{0,1:T(8,128)S(1)} %copy-done.1, s32[1024]{0:T(1024)S(1)} %bitcast.16), kind=kCustom, calls=%fused_computation | custom fusion | bytes 16384 | tf_op jit(solution)/shard_map/jit(take_along_axis)/gather | solution.py:14
  16.4 0.1 add.65
  16.5 130.7 %all-gather.2.cloned.1.call-done = bf16[1024,768]{1,0:T(8,128)(2,1)} async-done(((bf16[32,768]{1,0:T(8,128)(2,1)}), bf16[1024,768]{1,0:T(8,128)(2,1)}) %all-gather.2.cloned.1.call-update) | async-done | bytes 1572880 | tf_op jit(solution)/shard_map/all_gather | solution.py:18
  147.2 3.2 broadcast_in_dim.26
  150.4 4.1 select_convert_fusion
  154.5 1.3 copy-done.4
  155.9 3.6 fusion.7
  159.4 0.0 all-reduce.2.cloned.1.call-update
  159.5 0.0 reduce-scatter.2.cloned.1.call-start
  159.5 5.1 %fusion.6 = f32[1024,768]{1,0:T(8,128)} fusion(bf16[1024,1024]{1,0:T(8,128)(2,1)} %copy-done.4, bf16[1024,768]{1,0:T(8,128)(2,1)S(1)} %copy-done), kind=kOutput, calls=%fused_computation.23 | convolution fusion | flops 1610612736 | bytes 6815744 | tf_op jit(solution)/shard_map/dot_general | solution.py:25
  164.6 0.0 reduce-scatter.2.cloned.1.call-update
  164.6 147.7 %all-reduce.2.cloned.1.call-done = f32[1024,768]{1,0:T(8,128)} async-done(((f32[1024,768]{1,0:T(8,128)}), f32[1024,768]{1,0:T(8,128)}) %all-reduce.2.cloned.1.call-update) | async-done | bytes 3145744 | tf_op jit(solution)/shard_map/psum | solution.py:33
  312.3 3.3 multiply_convert_fusion
  315.6 147.1 %reduce-scatter.2.cloned.1.call-done = f32[32,768]{1,0:T(8,128)} async-done(((f32[1024,768]{1,0:T(8,128)}), f32[32,768]{1,0:T(8,128)}) %reduce-scatter.2.cloned.1.call-update) | async-done | bytes 98320 | tf_op jit(solution)/shard_map/reduce_scatter | solution.py:31
  (11 shorter events, 0.1 us)
Async XLA Ops:
  7.2 143.2 %copy-start = (bf16[1024,768]{1,0:T(8,128)(2,1)S(1)}, bf16[1024,768]{1,0:T(8,128)(2,1)}, u32[]{:S(2)}) copy-start(bf16[1024,768]{1,0:T(8,128)(2,1)} %param.5) | copy-start | bytes 4718596
  7.2 2.7 copy-start.1
  7.2 140.0 %all-gather.2.cloned.1.call-start = ((), (), s32[]{:S(2)}) async-start(), calls=%async_computation.1 | async-start | bytes 1622016 | tf_op jit(solution)/shard_map/all_gather | solution.py:18
  7.9 304.4 %all-reduce.2.cloned.1.call-start = ((), (), s32[]{:S(2)}) async-start(), calls=%async_computation.3 | async-start | bytes 6291456 | tf_op jit(solution)/shard_map/psum | solution.py:33
  9.9 6.6 %copy-start.2 = (s32[1024]{0:T(1024)S(1)}, s32[1024]{0:T(1024)}, u32[]{:S(2)}) copy-start(s32[1024]{0:T(1024)} %param.7) | copy-start | bytes 12292
  150.4 5.5 %copy-start.3 = (bf16[1024,768]{1,0:T(8,128)(2,1)S(1)}, bf16[1024,768]{1,0:T(8,128)(2,1)}, u32[]{:S(2)}) copy-start(bf16[1024,768]{1,0:T(8,128)(2,1)} %all-gather.2.cloned.1.call-done) | copy-start | bytes 4718596
  154.5 1.3 copy-start.4
  159.5 303.2 %reduce-scatter.2.cloned.1.call-start = ((), (), s32[]{:S(2)}) async-start(), calls=%async_computation.2 | async-start | bytes 3244032 | tf_op jit(solution)/shard_map/reduce_scatter | solution.py:31
Sparse Core Ops, SparseCore 0:
  10.1 137.0 all-gather.1
  159.6 152.6 all-reduce.1
  315.7 146.9 reduce-scatter.1
where the time goes:
time: 469 us
  waiting for transfers between devices  426 us (91%)
  between operations  13.9 us (3%)
  matrix products  12.8 us (3%)
  local copies, waits for them, and re-layouts  11.4 us (2%)
  other arithmetic  4.9 us (1%)
    psum x1, waiting for transfers between devices, shards(): total = lax.psum(w_acc, 'pb')  148 us
    reduce_scatter x1, waiting for transfers between devices, shards(): lax.psum_scatter(dq_all, 'lab', scatter_dimension=0, tiled=True)  147 us
    all_gather x1, waiting for transfers between devices, shards(): piece = lax.all_gather(queries, 'lab', axis=0, tiled=True)  131 us
  transfers between devices with their start and end apart: 3, of which 3 were waited for; matrix products, arithmetic and copies ran while one was open for 4% of the time, Pallas kernels for 0%

commit v1 on v0

v1 whole, which is shorter than its diff:
```python
import functools

import jax
import jax.numpy as jnp
from jax import lax
from jax.experimental import pallas as pl
from jax.experimental.pallas import tpu as pltpu
from jax.sharding import PartitionSpec as P

MESH = pl.DeviceIdType.MESH
BLOCK = 128
F32 = jnp.float32
BF16 = jnp.bfloat16


def mm(a, b, ca=1, cb=0):
    return lax.dot_general(a, b, (((ca,), (cb,)), ((), ())), preferred_element_type=F32)


def kernel(n_pb, n_lab, q_ref, w_ref, sib_ref, pos_ref, dq_ref, wg_ref, sbuf, rbuf, xbuf, pown, meta, meta_x, sbuf2, rbuf2,
           dwbuf, dwrecv, fin, s1, r1, sx, rx, s2, r2, s3, r3, s4, r4, s5, r5):
    runs, rows = sib_ref.shape[1], sib_ref.shape[2]
    kk = sib_ref.shape[0]
    cap = rows * kk // n_lab
    slots = n_lab * cap
    dim = q_ref.shape[1]
    labels = w_ref.shape[0]
    nblk = labels // BLOCK
    half = labels // 2
    chips = n_pb // 2
    piece = half // chips
    nz = n_lab // 2
    p = lax.axis_index("pb")
    me = lax.axis_index("lab")
    core = lax.rem(p, 2)
    chip = lax.div(p, 2)
    partner = p + 1 - 2 * core
    my_y = lax.div(me, nz)
    my_z = lax.rem(me, nz)

    def peer(t):
        back = n_lab - 1 - t
        step = lax.div(back, 2)
        dist = lax.div(step + 1, 2)
        dz = jnp.where(lax.rem(step, 2) == 1, dist, -dist)
        z = lax.rem(my_z + dz + nz, nz)
        y = lax.rem(my_y + lax.rem(back, 2), 2)
        return y * nz + z

    barrier = pltpu.get_barrier_semaphore()
    pl.semaphore_signal(barrier, inc=1, device_id=(partner, me), device_id_type=MESH)

    def sig_lab(t, c):
        pl.semaphore_signal(barrier, inc=1, device_id=(p, peer(t)), device_id_type=MESH)
        return c

    lax.fori_loop(0, n_lab - 1, sig_lab, 0)

    def sig_pb(t, c):
        other = lax.rem(chip + t, chips)
        pl.semaphore_signal(barrier, inc=1, device_id=(2 * other + core, me), device_id_type=MESH)
        return c

    lax.fori_loop(1, chips, sig_pb, 0)

    iota = lambda shape, ax: lax.broadcasted_iota(jnp.int32, shape, ax)
    expand = (iota((slots, n_lab), 0) // cap == iota((slots, n_lab), 1)).astype(BF16)
    upper = (iota((rows, rows), 0) <= iota((rows, rows), 1)).astype(BF16)
    rank_want = (lax.rem(iota((slots, rows), 0), cap) + 1).astype(F32)

    def pick(hit):
        hit_b = hit.astype(BF16)
        rank = mm(hit_b, upper)
        hx = mm(expand, hit_b)
        rx_ = mm(expand, rank.astype(BF16))
        return jnp.logical_and(hx > 0.5, rx_ == rank_want)

    run_id = iota((n_lab, rows), 0)
    hit_own = jnp.zeros((n_lab, rows), F32)
    for k in range(kk):
        row = sib_ref[k, pl.ds(me, 1), :]
        hit_own = jnp.where(jnp.right_shift(row, 3) == run_id, 1.0, hit_own)
    sel_own = jnp.where(pick(hit_own), 1.0, 0.0).astype(BF16)
    pown[...] = sel_own
    sent = mm(sel_own, q_ref[...])
    sbuf[...] = sent.reshape(n_lab, cap, dim).astype(BF16)

    pl.semaphore_wait(barrier, n_lab - 1 + chips - 1 + 1)

    def copy1(to, src_of):
        return pltpu.make_async_remote_copy(
            src_ref=sbuf.at[to], dst_ref=rbuf.at[src_of], send_sem=s1.at[to], recv_sem=r1.at[src_of],
            device_id=(p, to), device_id_type=MESH)

    def send1(t, c):
        copy1(peer(t), me).start()
        return c

    lax.fori_loop(0, n_lab - 1, send1, 0)
    rbuf[pl.ds(me, 1)] = sbuf[pl.ds(me, 1)]

    pos = pos_ref[...]
    hit_lab = jnp.zeros((runs, rows), F32)
    blk = jnp.zeros((runs, rows), F32)
    pblock = jnp.zeros((runs, rows), jnp.int32)
    for k in range(kk):
        sk = sib_ref[k]
        mine = jnp.right_shift(sk, 3) == me
        hit_lab = jnp.where(mine, 1.0, hit_lab)
        blk = jnp.where(mine, jnp.bitwise_and(sk, 7).astype(F32), blk)
        pblock = jnp.where(jnp.right_shift(pos, 7) == k, sk, pblock)
    pcol = jnp.where(jnp.right_shift(pblock, 3) == me, jnp.bitwise_and(pos, BLOCK - 1), -1).astype(F32)
    sel_lab = pick(hit_lab)
    blk_s = jnp.sum(jnp.where(sel_lab, mm(expand, blk.astype(BF16)), 0.0), axis=1, keepdims=True)
    pc_s = jnp.sum(jnp.where(sel_lab, mm(expand, pcol.astype(BF16)), 0.0), axis=1, keepdims=True)
    lane = iota((slots, BLOCK), 1)
    meta[...] = jnp.where(lane == 0, blk_s, pc_s)
    fwd_meta = pltpu.make_async_remote_copy(
        src_ref=meta, dst_ref=meta_x, send_sem=sx.at[0], recv_sem=rx.at[0], device_id=(partner, me), device_id_type=MESH)
    fwd_meta.start()

    def wait1(t, c):
        copy1(peer(t), peer(t)).wait_recv()
        return c

    lax.fori_loop(0, n_lab - 1, wait1, 0)
    fwd_rows = pltpu.make_async_remote_copy(
        src_ref=rbuf, dst_ref=xbuf, send_sem=sx.at[1], recv_sem=rx.at[1], device_id=(partner, me), device_id_type=MESH)
    fwd_rows.start()

    lane_f = lane.astype(F32)

    def slope128(x, w, b_of, pc, n):
        scores = mm(x, w, 1, 1)
        acc = jnp.zeros((slots, BLOCK), F32)
        for b in range(n):
            acc = jnp.where(b_of == float(b), scores[:, b * BLOCK:(b + 1) * BLOCK], acc)
        return jax.nn.sigmoid(acc) - jnp.where(lane_f == pc, 1.0, 0.0)

    def spread(sl, b_of, n):
        return jnp.concatenate([jnp.where(b_of == float(b), sl, 0.0) for b in range(n)], axis=1).astype(BF16)

    x = rbuf[...].astype(F32).reshape(slots, dim).astype(BF16)
    sl = slope128(x, w_ref[...], blk_s, pc_s, nblk)
    dq_part = mm(spread(sl, blk_s, nblk), w_ref[...])
    sbuf2[...] = dq_part.reshape(n_lab, cap, dim).astype(BF16)

    def copy2(to, src_of):
        return pltpu.make_async_remote_copy(
            src_ref=sbuf2.at[to], dst_ref=rbuf2.at[src_of], send_sem=s2.at[to], recv_sem=r2.at[src_of],
            device_id=(p, to), device_id_type=MESH)

    def send2(t, c):
        copy2(peer(t), me).start()
        return c

    lax.fori_loop(0, n_lab - 1, send2, 0)
    rbuf2[pl.ds(me, 1)] = sbuf2[pl.ds(me, 1)]

    hblk = nblk // 2
    first = core.astype(F32) * hblk
    own_half = spread(sl, blk_s - first, hblk)
    dw = mm(own_half, x, 0, 0)
    fwd_meta.wait_recv()
    fwd_rows.wait_recv()
    x2 = xbuf[...].astype(F32).reshape(slots, dim).astype(BF16)
    m2 = meta_x[...]
    b2 = m2[:, 0:1] - first
    pc2 = m2[:, 1:2]
    w_half = w_ref[pl.ds(pl.multiple_of(core * half, half), half), :]
    sl2 = slope128(x2, w_half, b2, pc2, hblk)
    dw = dw + mm(spread(sl2, b2, hblk), x2, 0, 0)
    dwbuf[...] = dw.astype(BF16).reshape(chips, piece, dim)

    def copy3(to, src_of):
        return pltpu.make_async_remote_copy(
            src_ref=dwbuf.at[to], dst_ref=dwrecv.at[src_of], send_sem=s3.at[to], recv_sem=r3.at[src_of],
            device_id=(2 * to + core, me), device_id_type=MESH)

    def send3(t, c):
        copy3(lax.rem(chip + t, chips), chip).start()
        return c

    lax.fori_loop(1, chips, send3, 0)
    dwrecv[pl.ds(chip, 1)] = dwbuf[pl.ds(chip, 1)]

    def wait3(t, c):
        other = lax.rem(chip + t, chips)
        copy3(other, other).wait_recv()
        return c

    lax.fori_loop(1, chips, wait3, 0)
    total = dwrecv[0].astype(F32)
    for j in range(1, chips):
        total = total + dwrecv[j].astype(F32)
    done = (total / n_pb).astype(BF16)
    fin[...] = done

    def rows_of(c_, j):
        return pl.ds(pl.multiple_of(c_ * half + j * piece, piece), piece)

    wg_ref[rows_of(core, chip), :] = done

    def copy4(to, src_of):
        return pltpu.make_async_remote_copy(
            src_ref=fin, dst_ref=wg_ref.at[rows_of(core, src_of)], send_sem=s4.at[to], recv_sem=r4.at[src_of],
            device_id=(2 * to + core, me), device_id_type=MESH)

    def send4(t, c):
        copy4(lax.rem(chip + t, chips), chip).start()
        return c

    lax.fori_loop(1, chips, send4, 0)
    to_partner = pltpu.make_async_remote_copy(
        src_ref=fin, dst_ref=wg_ref.at[rows_of(core, chip)], send_sem=s5.at[chip], recv_sem=r5.at[chip],
        device_id=(partner, me), device_id_type=MESH)
    to_partner.start()

    def wait2(t, c):
        copy2(peer(t), peer(t)).wait_recv()
        return c

    lax.fori_loop(0, n_lab - 1, wait2, 0)
    back = rbuf2[...].astype(F32).reshape(slots, dim).astype(BF16)
    dq_ref[...] = mm(pown[...], back, 0, 0)

    def copy5(c_, j):
        return pltpu.make_async_remote_copy(
            src_ref=wg_ref.at[rows_of(c_, j)], dst_ref=wg_ref.at[rows_of(c_, j)], send_sem=s5.at[j], recv_sem=r5.at[j],
            device_id=(partner, me), device_id_type=MESH)

    def relay(t, c):
        other = lax.rem(chip + t, chips)
        copy4(other, other).wait_recv()
        copy5(core, other).start()
        return c

    lax.fori_loop(1, chips, relay, 0)

    def wait5(j, c):
        copy5(1 - core, j).wait_recv()
        return c

    lax.fori_loop(0, chips, wait5, 0)

    def drain_lab(t, c):
        copy1(peer(t), me).wait_send()
        copy2(peer(t), me).wait_send()
        return c

    lax.fori_loop(0, n_lab - 1, drain_lab, 0)

    def drain_pb(t, c):
        other = lax.rem(chip + t, chips)
        copy3(other, chip).wait_send()
        copy4(other, chip).wait_send()
        copy5(core, other).wait_send()
        return c

    lax.fori_loop(1, chips, drain_pb, 0)
    to_partner.wait_send()
    fwd_meta.wait_send()
    fwd_rows.wait_send()


def shards(n_pb, n_lab, queries, label_weights, sibling_blocks, positive_slot):
    rows, dim = queries.shape
    labels = label_weights.shape[0]
    kk = sibling_blocks.shape[1]
    runs = sibling_blocks.shape[0] // rows
    cap = rows * kk // n_lab
    slots = n_lab * cap
    chips = n_pb // 2
    piece = labels // 2 // chips
    sib = sibling_blocks.T.reshape(kk, runs, rows)
    pos = positive_slot.reshape(runs, rows)
    vmem = pl.BlockSpec(memory_space=pltpu.VMEM)
    dma = pltpu.SemaphoreType.DMA
    packets = pltpu.VMEM((n_lab, cap, dim), BF16)
    return pl.pallas_call(
        functools.partial(kernel, n_pb, n_lab),
        out_shape=(jax.ShapeDtypeStruct((rows, dim), F32), jax.ShapeDtypeStruct((labels, dim), BF16)),
        in_specs=[vmem] * 4,
        out_specs=(vmem, vmem),
        scratch_shapes=[
            packets, packets, packets, pltpu.VMEM((slots, rows), BF16),
            pltpu.VMEM((slots, BLOCK), F32), pltpu.VMEM((slots, BLOCK), F32), packets, packets,
            pltpu.VMEM((chips, piece, dim), BF16), pltpu.VMEM((chips, piece, dim), BF16), pltpu.VMEM((piece, dim), BF16),
            dma((n_lab,)), dma((n_lab,)), dma((2,)), dma((2,)), dma((n_lab,)), dma((n_lab,)),
            dma((chips,)), dma((chips,)), dma((chips,)), dma((chips,)), dma((chips,)), dma((chips,)),
        ],
        compiler_params=pltpu.CompilerParams(collective_id=0, has_side_effects=True),
    )(queries, label_weights, sib, pos)


def solution(mesh):
    in_specs = (P(("pb", "lab"), None), P("lab", None), P("pb", None), P("pb"))
    out_specs = (P(("pb", "lab"), None), P("lab", None))
    body = functools.partial(shards, mesh.shape["pb"], mesh.shape["lab"])
    return jax.shard_map(body, mesh=mesh, in_specs=in_specs, out_specs=out_specs, check_vma=False)
```

time: 469 us -> 77.8 us (0.17)
  the two profiles are of different devices: /device:TPU:6 before, /device:TPU:1 now
where the time goes in v1:
time: 77.8 us; the launch traced here: 77.5 us
  Pallas kernels  69.8 us (90%)
  local copies, waits for them, and re-layouts  7.06 us (9%)
    pallas_call x1, Pallas kernels, shards(): pl.pallas_call(functools.partial(kernel, n_pb, n_lab), out_shape=(jax.Sha...  69.8 us
    unnamed x2, local copies, waits for them, and re-layouts  4.19 us

profile of v1, /device:TPU:1, one launch (start us, length us, event | category | flops | bytes accessed | tf_op | source)
XLA Modules:
  0.0 77.5 jit_solution(5252523077245405606)
XLA Ops:
  0.6 1.4 %reshape.11.pos_ref = s32[32,32]{1,0:T(8,128)} reshape(s32[1024]{0:T(1024)} %param.7) | data formatting | bytes 8192 | tf_op jit(solution)/shard_map/reshape | solution.py:276
  2.0 1.5 %reshape.10.sib_ref = s32[8,32,32]{2,1,0:T(8,128)} reshape(s32[8,1024]{1,0:T(8,128)} %bitcast.1) | data formatting | bytes 65536 | tf_op jit(solution)/shard_map/reshape | solution.py:275
  3.5 69.8 %shard_map.59 = (f32[32,768]{1,0:T(8,128)}, bf16[1024,768]{1,0:T(8,128)(2,1)}) custom-call(bf16[32,768]{1,0:T(8,128)(2,1)} %q_ref.1, bf16[1024,768]{1,0:T(8,128)(2,1)} %w_ref.1, s32[8,32,32]{2,1,0:T(8,128)} %reshape.10.sib_ref, s32[32,32]{1,0:T(8,128)} %reshape.11.pos_ref), custom_call_target="tpu_custom_call" | custom-call | tf_op jit(solution)/shard_map/pallas_call | solution.py:280
  73.4 1.5 %copy.8 = f32[32,768]{1,0:T(8,128)} copy(f32[32,768]{1,0:T(8,128)} %get-tuple-element.4) | data formatting | bytes 196608
  74.9 2.7 %copy.9 = bf16[1024,768]{1,0:T(8,128)(2,1)} copy(bf16[1024,768]{1,0:T(8,128)(2,1)} %get-tuple-element.5) | data formatting | bytes 3145728

commit v2 on v0

v2 whole, which is shorter than its diff:
```python
import functools

import jax
import jax.numpy as jnp
from jax import lax
from jax.experimental import pallas as pl
from jax.experimental.pallas import tpu as pltpu
from jax.sharding import PartitionSpec as P

MESH = pl.DeviceIdType.MESH
BLOCK = 128
HOP = 4
LIST = 16
F32 = jnp.float32
BF16 = jnp.bfloat16
SELF_NEAR = 2 * (HOP - 1)
N_NEAR = 2 * (2 * HOP - 1)
N_RELAY = 2 * HOP + 1


def mm(a, b, ca=1, cb=0):
    return lax.dot_general(a, b, (((ca,), (cb,)), ((), ())), preferred_element_type=F32)


def iota(shape, ax):
    return lax.broadcasted_iota(jnp.int32, shape, ax)


def kernel(n_pb, n_lab, q_ref, w_hbm, sib_ref, pos_ref, dq_ref, wg_ref, w_ref, sbuf, fbuf, relbuf, rbuf, xbuf, pown, prel, meta, meta_x,
           sbuf2, nbuf, rrbuf, fsend, fback, dwbuf, dwrecv, fin,
           sw, s1, r1, sf, rf, sr, sx, rx, s2, rn, rr, sb, rb, s3, r3, s4, r4, s5, r5):
    kk, total_rows = sib_ref.shape
    rows, dim = q_ref.shape
    cap = rows * kk // n_lab
    slots = n_lab * cap
    labels = w_hbm.shape[0]
    nblk = labels // BLOCK
    half = labels // 2
    chips = n_pb // 2
    piece = half // chips
    nz = n_lab // 2
    p = lax.axis_index("pb")
    me = lax.axis_index("lab")
    core = lax.rem(p, 2)
    chip = lax.div(p, 2)
    partner = p + 1 - 2 * core
    my_y = lax.div(me, nz)
    my_z = lax.rem(me, nz)

    def at(dy, dz):
        return lax.rem(my_y + dy, 2) * nz + lax.rem(my_z + dz + nz, nz)

    load_w = pltpu.make_async_copy(w_hbm, w_ref, sw)
    load_w.start()

    barrier = pltpu.get_barrier_semaphore()
    for dz in range(-HOP, HOP + 1):
        for dy in range(2):
            if dz or dy:
                pl.semaphore_signal(barrier, inc=1, device_id=(p, at(dy, dz)), device_id_type=MESH)
    pl.semaphore_signal(barrier, inc=1, device_id=(partner, me), device_id_type=MESH)
    for t in range(1, chips):
        pl.semaphore_signal(barrier, inc=1, device_id=(2 * lax.rem(chip + t, chips) + core, me), device_id_type=MESH)

    src_a, src_b = at(0, -HOP), at(0, HOP)
    upper = (iota((rows, rows), 0) <= iota((rows, rows), 1)).astype(BF16)

    def pick(hit_b, n):
        expand = (iota((n * cap, n), 0) // cap == iota((n * cap, n), 1)).astype(BF16)
        want = (lax.rem(iota((n * cap, rows), 0), cap) + 1).astype(F32)
        rank = mm(hit_b, upper)
        on = mm(expand, hit_b)
        return jnp.logical_and(on > 0.5, mm(expand, rank.astype(BF16)) == want), expand

    sib = sib_ref[...]
    col = iota((total_rows, 3 * rows), 1)
    run_of = jnp.where(col < rows, me, jnp.where(col < 2 * rows, src_a, src_b))
    take = (iota((total_rows, 3 * rows), 0) == run_of * rows + lax.rem(col, rows)).astype(BF16)
    mine3 = mm(sib.astype(BF16), take)

    jrow = iota((LIST, rows), 0)
    jy = lax.rem(jrow, 2)
    jm = lax.div(jrow, 2)

    def lab_of(dy, dz):
        return lax.rem(my_y + dy, 2) * nz + lax.rem(my_z + dz + nz, nz)

    near_ids = jnp.where(jrow < N_NEAR, lab_of(jy, jm - (HOP - 1)), -1)
    ids_a = jnp.where(jrow < N_RELAY, lab_of(jy, jm), -1)
    ids_b = jnp.where(jrow < N_RELAY, lab_of(jnp.where(jrow == N_RELAY - 1, 1, jy), -jm), -1)
    hits = []
    for n, ids in enumerate((near_ids, ids_a, ids_b)):
        hit = jnp.zeros((LIST, rows), F32)
        for k in range(kk):
            blocks = mine3[k:k + 1, n * rows:(n + 1) * rows].astype(jnp.int32)
            hit = jnp.where(jnp.right_shift(blocks, 3) == ids, 1.0, hit)
        hits.append(hit)
    sel3, _ = pick(jnp.concatenate(hits, axis=0).astype(BF16), 3 * LIST)
    sel3 = jnp.where(sel3, 1.0, 0.0).astype(BF16)
    width = LIST * cap
    pown[...] = sel3[:width]
    prel[...] = sel3[width:]
    sbuf[...] = mm(sel3[:width], q_ref[...]).reshape(LIST, cap, dim).astype(BF16)

    pl.semaphore_wait(barrier, 2 * (2 * HOP + 1) - 1 + chips)

    def remote(src, dst, send, recv, dev):
        return pltpu.make_async_remote_copy(
            src_ref=src, dst_ref=dst, send_sem=send, recv_sem=recv, device_id=dev, device_id_type=MESH)

    def chunk_out(s):
        return remote(q_ref, fbuf.at[s], sf.at[s], rf.at[s], (p, at(0, HOP if s == 0 else -HOP)))

    chunk_out(0).start()
    chunk_out(1).start()
    near = [(dz * sg, dy) for dz in range(HOP - 1, -1, -1) for sg in ((1, -1) if dz else (1,)) for dy in (0, 1) if dz or dy]
    for dz, dy in near:
        j = 2 * (dz + HOP - 1) + dy
        remote(sbuf.at[j], rbuf.at[me], s1.at[0], r1, (p, at(dy, dz))).start()
    rbuf[pl.ds(me, 1)] = sbuf[pl.ds(SELF_NEAR, 1)]

    qrow = iota((n_lab, total_rows), 1)
    in_run = jnp.right_shift(qrow, 5) == iota((n_lab, total_rows), 0)
    fold = (jnp.bitwise_and(iota((total_rows, rows), 0), rows - 1) == iota((total_rows, rows), 1)).astype(BF16)
    here = jnp.right_shift(sib, 3) == me
    pos = pos_ref[...]
    blk1 = jnp.sum(jnp.where(here, jnp.bitwise_and(sib, 7) + 1, 0), axis=0, keepdims=True)
    is_pos = jnp.logical_and(here, iota((kk, total_rows), 0) == jnp.right_shift(pos, 7))
    col1 = jnp.sum(jnp.where(is_pos, jnp.bitwise_and(pos, BLOCK - 1) + 1, 0), axis=0, keepdims=True)
    packed = jnp.concatenate([jnp.where(in_run, blk1, 0), jnp.where(in_run, col1, 0)], axis=0)
    table = mm(packed.astype(F32).astype(BF16), fold)
    blk_t, col_t = table[:n_lab], table[n_lab:]
    sel_lab, expand = pick(jnp.where(blk_t > 0.5, 1.0, 0.0).astype(BF16), n_lab)
    blk_s = jnp.sum(jnp.where(sel_lab, mm(expand, blk_t.astype(BF16)), 0.0), axis=1, keepdims=True) - 1.0
    pc_s = jnp.sum(jnp.where(sel_lab, mm(expand, col_t.astype(BF16)), 0.0), axis=1, keepdims=True) - 1.0
    lane = iota((slots, BLOCK), 1)
    meta[...] = jnp.where(lane == 0, blk_s, pc_s)
    fwd_meta = remote(meta, meta_x, sx.at[0], rx.at[0], (partner, me))
    fwd_meta.start()
    nbuf[N_NEAR:] = jnp.zeros((LIST - N_NEAR, cap, dim), BF16)
    rrbuf[0, N_RELAY:] = jnp.zeros((LIST - N_RELAY, cap, dim), BF16)
    rrbuf[1, N_RELAY:] = jnp.zeros((LIST - N_RELAY, cap, dim), BF16)

    def stop(s, jj):
        if jj == N_RELAY - 1:
            return (0, HOP) if s == 0 else (1, -HOP)
        m, dy = divmod(jj, 2)
        return dy, (m if s == 0 else -m)

    srcs = (src_a, src_b)
    for s in range(2):
        chunk_out(s).wait_recv()
        out = mm(prel[s * width:(s + 1) * width], fbuf[s])
        relbuf[s] = out.reshape(LIST, cap, dim).astype(BF16)
        for jj in range(N_RELAY - 1, 0, -1):
            dy, dz = stop(s, jj)
            remote(relbuf.at[s, jj], rbuf.at[srcs[s]], sr.at[s], r1, (p, at(dy, dz))).start()
        rbuf[pl.ds(srcs[s], 1)] = relbuf[s, 0:1]

    def bulk(ref, sem):
        return remote(ref, ref, sem, sem, (partner, me))

    n_in = n_lab - 3
    bulk(rbuf.at[pl.ds(0, n_in)], r1).wait_recv()
    fwd_rows = remote(rbuf, xbuf, sx.at[1], rx.at[1], (partner, me))
    fwd_rows.start()
    load_w.wait()

    lane_f = lane.astype(F32)

    def slope128(x, w, b_of, pc, n):
        scores = mm(x, w, 1, 1)
        acc = jnp.zeros((slots, BLOCK), F32)
        for b in range(n):
            acc = jnp.where(b_of == float(b), scores[:, b * BLOCK:(b + 1) * BLOCK], acc)
        return jax.nn.sigmoid(acc) - jnp.where(lane_f == pc, 1.0, 0.0)

    def spread(sl, b_of, n):
        return jnp.concatenate([jnp.where(b_of == float(b), sl, 0.0) for b in range(n)], axis=1).astype(BF16)

    x = rbuf[...].astype(F32).reshape(slots, dim).astype(BF16)
    sl = slope128(x, w_ref[...], blk_s, pc_s, nblk)
    dq_part = mm(spread(sl, blk_s, nblk), w_ref[...])
    sbuf2[...] = dq_part.reshape(n_lab, cap, dim).astype(BF16)

    for s in range(2):
        for jj in range(N_RELAY - 1, 0, -1):
            dy, dz = stop(s, jj)
            relay_dz = -dz
            home = at(dy, relay_dz - HOP if s == 0 else relay_dz + HOP)
            remote(sbuf2.at[home], rrbuf.at[s, jj], s2, rr.at[s], (p, at(dy, relay_dz))).start()
        rrbuf[s, 0:1] = sbuf2[pl.ds(srcs[s], 1)]
    for dz, dy in near:
        home = at(dy, dz)
        remote(sbuf2.at[home], nbuf.at[2 * (HOP - 1 - dz) + dy], s2, rn, (p, home)).start()
    nbuf[SELF_NEAR:SELF_NEAR + 1] = sbuf2[pl.ds(me, 1)]

    hblk = nblk // 2
    first = core.astype(F32) * hblk
    dw = mm(spread(sl, blk_s - first, hblk), x, 0, 0)
    fwd_meta.wait_recv()
    fwd_rows.wait_recv()
    x2 = xbuf[...].astype(F32).reshape(slots, dim).astype(BF16)
    m2 = meta_x[...]
    b2 = m2[:, 0:1] - first
    w_half = w_ref[pl.ds(pl.multiple_of(core * half, half), half), :]
    sl2 = slope128(x2, w_half, b2, m2[:, 1:2], hblk)
    dw = dw + mm(spread(sl2, b2, hblk), x2, 0, 0)
    dwbuf[...] = dw.astype(BF16).reshape(chips, piece, dim)
    for t in range(1, chips):
        to = lax.rem(chip + t, chips)
        remote(dwbuf.at[to], dwrecv.at[chip], s3, r3, (2 * to + core, me)).start()
    dwrecv[pl.ds(chip, 1)] = dwbuf[pl.ds(chip, 1)]

    def to_home(s):
        return remote(fsend.at[s], fback.at[s], sb.at[s], rb.at[s], (p, srcs[s]))

    for s in range(2):
        bulk(rrbuf.at[s, pl.ds(0, N_RELAY - 1)], rr.at[s]).wait_recv()
        terms = rrbuf[s].astype(F32).reshape(width, dim).astype(BF16)
        fsend[s] = mm(prel[s * width:(s + 1) * width], terms, 0, 0).astype(BF16)
        to_home(s).start()

    bulk(dwrecv.at[pl.ds(0, chips - 1)], r3).wait_recv()
    total = dwrecv[0].astype(F32)
    for j in range(1, chips):
        total = total + dwrecv[j].astype(F32)
    done = (total / n_pb).astype(BF16)
    fin[...] = done

    def rows_of(c_, j):
        return pl.ds(pl.multiple_of(c_ * half + j * piece, piece), piece)

    wg_ref[rows_of(core, chip), :] = done

    def share(to, j):
        return remote(fin, wg_ref.at[rows_of(core, j)], s4, r4.at[j], (2 * to + core, me))

    for t in range(1, chips):
        share(lax.rem(chip + t, chips), chip).start()
    remote(fin, wg_ref.at[rows_of(core, chip)], s5, r5, (partner, me)).start()

    bulk(nbuf.at[pl.ds(0, N_NEAR - 1)], rn).wait_recv()
    terms = nbuf[...].astype(F32).reshape(width, dim).astype(BF16)
    home_sum = mm(pown[...], terms, 0, 0)
    for s in range(2):
        to_home(s).wait_recv()
        home_sum = home_sum + fback[s].astype(F32)
    dq_ref[...] = home_sum

    for t in range(1, chips):
        other = lax.rem(chip + t, chips)
        share(other, other).wait_recv()
        there = wg_ref.at[rows_of(core, other)]
        remote(there, there, s5, r5, (partner, me)).start()
    bulk(wg_ref.at[pl.ds(pl.multiple_of((1 - core) * half, half), half)], r5).wait_recv()

    bulk(sbuf.at[pl.ds(0, N_NEAR - 1)], s1.at[0]).wait_send()
    for s in range(2):
        chunk_out(s).wait_send()
        bulk(relbuf.at[s, pl.ds(0, N_RELAY - 1)], sr.at[s]).wait_send()
        to_home(s).wait_send()
    fwd_meta.wait_send()
    fwd_rows.wait_send()
    bulk(sbuf2.at[pl.ds(0, n_in)], s2).wait_send()
    bulk(dwbuf.at[pl.ds(0, chips - 1)], s3).wait_send()
    bulk(dwbuf.at[pl.ds(0, chips - 1)], s4).wait_send()
    bulk(wg_ref.at[pl.ds(pl.multiple_of(core * half, half), half)], s5).wait_send()


def write_out(a_ref, b_ref, oa_ref, ob_ref, sems):
    first = pltpu.make_async_copy(b_ref, ob_ref, sems.at[0])
    second = pltpu.make_async_copy(a_ref, oa_ref, sems.at[1])
    first.start()
    second.start()
    first.wait()
    second.wait()


def shards(n_pb, n_lab, queries, label_weights, sibling_blocks, positive_slot):
    rows, dim = queries.shape
    labels = label_weights.shape[0]
    kk = sibling_blocks.shape[1]
    cap = rows * kk // n_lab
    slots = n_lab * cap
    chips = n_pb // 2
    piece = labels // 2 // chips
    width = LIST * cap
    sib = sibling_blocks.T
    pos = positive_slot.reshape(1, -1)
    vmem = pl.BlockSpec(memory_space=pltpu.VMEM)
    hbm = pl.BlockSpec(memory_space=pl.ANY)
    dma = pltpu.SemaphoreType.DMA

    def buf(*lead):
        return pltpu.VMEM((*lead, dim), BF16)

    dq, wg = pl.pallas_call(
        functools.partial(kernel, n_pb, n_lab),
        out_shape=(pltpu.VMEM((rows, dim), F32), pltpu.VMEM((labels, dim), BF16)),
        in_specs=[vmem, hbm, vmem, vmem],
        out_specs=(vmem, vmem),
        scratch_shapes=[
            buf(labels), buf(LIST, cap), buf(2, rows), buf(2, LIST, cap), buf(n_lab, cap), buf(n_lab, cap),
            pltpu.VMEM((width, rows), BF16), pltpu.VMEM((2 * width, rows), BF16),
            pltpu.VMEM((slots, BLOCK), F32), pltpu.VMEM((slots, BLOCK), F32),
            buf(n_lab, cap), buf(LIST, cap), buf(2, LIST, cap), buf(2, rows), buf(2, rows),
            buf(chips, piece), buf(chips, piece), buf(piece),
            dma, dma((1,)), dma, dma((2,)), dma((2,)), dma((2,)), dma((2,)), dma((2,)), dma, dma, dma((2,)), dma((2,)), dma((2,)),
            dma, dma, dma, dma((chips,)), dma, dma,
        ],
        compiler_params=pltpu.CompilerParams(collective_id=0, has_side_effects=True),
    )(queries, label_weights, sib, pos)
    near = functools.partial(pltpu.with_memory_space_constraint, memory_space=pltpu.VMEM)
    return pl.pallas_call(
        write_out,
        out_shape=(jax.ShapeDtypeStruct((rows, dim), F32), jax.ShapeDtypeStruct((labels, dim), BF16)),
        in_specs=[vmem, vmem],
        out_specs=(hbm, hbm),
        scratch_shapes=[dma((2,))],
    )(near(dq), near(wg))


def solution(mesh):
    in_specs = (P(("pb", "lab"), None), P("lab", None), P("pb", None), P("pb"))
    out_specs = (P(("pb", "lab"), None), P("lab", None))
    body = functools.partial(shards, mesh.shape["pb"], mesh.shape["lab"])
    return jax.shard_map(body, mesh=mesh, in_specs=in_specs, out_specs=out_specs, check_vma=False)
```

time: 469 us -> 63.2 us (0.13)
  the two profiles are of different devices: /device:TPU:6 before, /device:TPU:1 now
where the time goes in v2:
time: 63.2 us; the launch traced here: 63 us
  Pallas kernels  62.4 us (99%)
  between operations  0.64 us (1%)
    pallas_call x1, Pallas kernels, shards(): pl.pallas_call(functools.partial(kernel, n_pb, n_lab), out_shape=(pltpu.V...  61.2 us

profile of v2, /device:TPU:1, one launch (start us, length us, event | category | flops | bytes accessed | tf_op | source)
XLA Modules:
  0.0 63.0 jit_solution(5343116784463362035)
XLA Ops:
  0.6 61.2 %shard_map.59 = (f32[32,768]{1,0:T(8,128)S(1)}, bf16[1024,768]{1,0:T(8,128)(2,1)S(1)}) custom-call(bf16[32,768]{1,0:T(8,128)(2,1)} %q_ref.1, bf16[1024,768]{1,0:T(8,128)(2,1)} %w_hbm.1, s32[8,1024]{1,0:T(8,128)} %bitcast.2, s32[1,1024]{1,0:T(1,128)} %bitcast.3), custom_call_target="tpu_custom_call" | custom-call | tf_op jit(solution)/shard_map/pallas_call | solution.py:298
  61.9 1.2 %shard_map.60 = (f32[32,768]{1,0:T(8,128)}, bf16[1024,768]{1,0:T(8,128)(2,1)}) custom-call(f32[32,768]{1,0:T(8,128)S(1)} %get-tuple-element.4.a_ref, bf16[1024,768]{1,0:T(8,128)(2,1)S(1)} %get-tuple-element.5.b_ref), custom_call_target="tpu_custom_call" | custom-call | tf_op jit(solution)/shard_map/pallas_call | solution.py:315

commit v3 on v2

--- a/solution.py
+++ b/solution.py
@@ -11,6 +11,7 @@
 BLOCK = 128
 HOP = 4
 LIST = 16
+PARTS = 2
 F32 = jnp.float32
 BF16 = jnp.bfloat16
 SELF_NEAR = 2 * (HOP - 1)
@@ -26,9 +27,9 @@
     return lax.broadcasted_iota(jnp.int32, shape, ax)
 
 
-def kernel(n_pb, n_lab, q_ref, w_hbm, sib_ref, pos_ref, dq_ref, wg_ref, w_ref, sbuf, fbuf, relbuf, rbuf, xbuf, pown, prel, meta, meta_x,
+def kernel(n_pb, n_lab, q_ref, w_hbm, sib_ref, pos_ref, dq_ref, wg_ref, w_ref, sbuf, fbuf, relbuf, rbuf, xall, sall, slb, pown, prel, meta, meta_x,
            sbuf2, nbuf, rrbuf, fsend, fback, dwbuf, dwrecv, fin,
-           sw, s1, r1, sf, rf, sr, sx, rx, s2, rn, rr, sb, rb, s3, r3, s4, r4, s5, r5):
+           sw, s1, rnear, rfar, sf, rf, sr, sx, rx, s2, rn, rr, sb, rb, s3, r3, s4, r4, s5, r5):
     kk, total_rows = sib_ref.shape
     rows, dim = q_ref.shape
     cap = rows * kk // n_lab
@@ -37,7 +38,8 @@
     nblk = labels // BLOCK
     half = labels // 2
     chips = n_pb // 2
-    piece = half // chips
+    part = half // PARTS
+    piece = part // chips
     nz = n_lab // 2
     p = lax.axis_index("pb")
     me = lax.axis_index("lab")
@@ -65,12 +67,11 @@
     src_a, src_b = at(0, -HOP), at(0, HOP)
     upper = (iota((rows, rows), 0) <= iota((rows, rows), 1)).astype(BF16)
 
-    def pick(hit_b, n):
-        expand = (iota((n * cap, n), 0) // cap == iota((n * cap, n), 1)).astype(BF16)
-        want = (lax.rem(iota((n * cap, rows), 0), cap) + 1).astype(F32)
+    def pick(hit_b, expand):
+        want = (lax.rem(iota((expand.shape[0], rows), 0), cap) + 1).astype(F32)
         rank = mm(hit_b, upper)
         on = mm(expand, hit_b)
-        return jnp.logical_and(on > 0.5, mm(expand, rank.astype(BF16)) == want), expand
+        return jnp.logical_and(on > 0.5, mm(expand, rank.astype(BF16)) == want)
 
     sib = sib_ref[...]
     col = iota((total_rows, 3 * rows), 1)
@@ -95,7 +96,8 @@
             blocks = mine3[k:k + 1, n * rows:(n + 1) * rows].astype(jnp.int32)
             hit = jnp.where(jnp.right_shift(blocks, 3) == ids, 1.0, hit)
         hits.append(hit)
-    sel3, _ = pick(jnp.concatenate(hits, axis=0).astype(BF16), 3 * LIST)
+    lists = 3 * LIST
+    sel3 = pick(jnp.concatenate(hits, axis=0).astype(BF16), (iota((lists * cap, lists), 0) // cap == iota((lists * cap, lists), 1)).astype(BF16))
     sel3 = jnp.where(sel3, 1.0, 0.0).astype(BF16)
     width = LIST * cap
     pown[...] = sel3[:width]
@@ -116,8 +118,8 @@
     near = [(dz * sg, dy) for dz in range(HOP - 1, -1, -1) for sg in ((1, -1) if dz else (1,)) for dy in (0, 1) if dz or dy]
     for dz, dy in near:
         j = 2 * (dz + HOP - 1) + dy
-        remote(sbuf.at[j], rbuf.at[me], s1.at[0], r1, (p, at(dy, dz))).start()
-    rbuf[pl.ds(me, 1)] = sbuf[pl.ds(SELF_NEAR, 1)]
+        remote(sbuf.at[j], rbuf.at[2 * (HOP - 1 - dz) + dy], s1.at[0], rnear, (p, at(dy, dz))).start()
+    rbuf[SELF_NEAR:SELF_NEAR + 1] = sbuf[SELF_NEAR:SELF_NEAR + 1]
 
     qrow = iota((n_lab, total_rows), 1)
     in_run = jnp.right_shift(qrow, 5) == iota((n_lab, total_rows), 0)
@@ -130,7 +132,15 @@
     packed = jnp.concatenate([jnp.where(in_run, blk1, 0), jnp.where(in_run, col1, 0)], axis=0)
     table = mm(packed.astype(F32).astype(BF16), fold)
     blk_t, col_t = table[:n_lab], table[n_lab:]
-    sel_lab, expand = pick(jnp.where(blk_t > 0.5, 1.0, 0.0).astype(BF16), n_lab)
+    slot = jnp.right_shift(iota((slots, n_lab), 0), 3)
+    jj_of = jnp.where(slot < LIST + N_RELAY - 1, slot - (LIST - 1), slot - (LIST + N_RELAY - 2))
+    far_a = lab_of(jnp.bitwise_and(jj_of, 1), -HOP - jnp.right_shift(jj_of, 1))
+    far_b = lab_of(jnp.where(jj_of == N_RELAY - 1, 1, jnp.bitwise_and(jj_of, 1)), HOP + jnp.right_shift(jj_of, 1))
+    source = jnp.where(slot < LIST + N_RELAY - 1, far_a, far_b)
+    source = jnp.where(slot == N_NEAR, src_a, jnp.where(slot == N_NEAR + 1, src_b, source))
+    source = jnp.where(slot < N_NEAR, lab_of(jnp.bitwise_and(slot, 1), jnp.right_shift(slot, 1) - (HOP - 1)), source)
+    expand = (source == iota((slots, n_lab), 1)).astype(BF16)
+    sel_lab = pick(jnp.where(blk_t > 0.5, 1.0, 0.0).astype(BF16), expand)
     blk_s = jnp.sum(jnp.where(sel_lab, mm(expand, blk_t.astype(BF16)), 0.0), axis=1, keepdims=True) - 1.0
     pc_s = jnp.sum(jnp.where(sel_lab, mm(expand, col_t.astype(BF16)), 0.0), axis=1, keepdims=True) - 1.0
     lane = iota((slots, BLOCK), 1)
@@ -147,6 +157,9 @@
         m, dy = divmod(jj, 2)
         return dy, (m if s == 0 else -m)
 
+    def far_slot(s, jj):
+        return LIST + s * (N_RELAY - 1) + jj - 1
+
     srcs = (src_a, src_b)
     for s in range(2):
         chunk_out(s).wait_recv()
@@ -154,23 +167,20 @@
         relbuf[s] = out.reshape(LIST, cap, dim).astype(BF16)
         for jj in range(N_RELAY - 1, 0, -1):
             dy, dz = stop(s, jj)
-            remote(relbuf.at[s, jj], rbuf.at[srcs[s]], sr.at[s], r1, (p, at(dy, dz))).start()
-        rbuf[pl.ds(srcs[s], 1)] = relbuf[s, 0:1]
+            remote(relbuf.at[s, jj], rbuf.at[far_slot(s, jj)], sr.at[s], rfar, (p, at(dy, dz))).start()
+        rbuf[N_NEAR + s:N_NEAR + s + 1] = relbuf[s, 0:1]
 
     def bulk(ref, sem):
         return remote(ref, ref, sem, sem, (partner, me))
 
-    n_in = n_lab - 3
-    bulk(rbuf.at[pl.ds(0, n_in)], r1).wait_recv()
-    fwd_rows = remote(rbuf, xbuf, sx.at[1], rx.at[1], (partner, me))
-    fwd_rows.start()
-    load_w.wait()
-
-    lane_f = lane.astype(F32)
+    hrows = slots // 2
+    hblk = nblk // 2
+    first = core.astype(F32) * hblk
+    lane_f = iota((hrows, BLOCK), 1).astype(F32)
 
     def slope128(x, w, b_of, pc, n):
         scores = mm(x, w, 1, 1)
-        acc = jnp.zeros((slots, BLOCK), F32)
+        acc = jnp.zeros((hrows, BLOCK), F32)
         for b in range(n):
             acc = jnp.where(b_of == float(b), scores[:, b * BLOCK:(b + 1) * BLOCK], acc)
         return jax.nn.sigmoid(acc) - jnp.where(lane_f == pc, 1.0, 0.0)
@@ -178,39 +188,64 @@
     def spread(sl, b_of, n):
         return jnp.concatenate([jnp.where(b_of == float(b), sl, 0.0) for b in range(n)], axis=1).astype(BF16)
 
-    x = rbuf[...].astype(F32).reshape(slots, dim).astype(BF16)
-    sl = slope128(x, w_ref[...], blk_s, pc_s, nblk)
-    dq_part = mm(spread(sl, blk_s, nblk), w_ref[...])
-    sbuf2[...] = dq_part.reshape(n_lab, cap, dim).astype(BF16)
-
+    def fwd_rows(hf):
+        return remote(xall.at[pl.ds(hf * hrows, hrows)], xall.at[pl.ds(slots + hf * hrows, hrows)], sx.at[1 + hf], rx.at[1 + hf], (partner, me))
+
+    def own_rows(hf):
+        x = rbuf[hf * LIST:(hf + 1) * LIST].astype(F32).reshape(hrows, dim).astype(BF16)
+        xall[hf * hrows:(hf + 1) * hrows] = x
+        fwd_rows(hf).start()
+        b_of = meta[hf * hrows:(hf + 1) * hrows, 0:1]
+        sl = slope128(x, w_ref[...], b_of, meta[hf * hrows:(hf + 1) * hrows, 1:2], nblk)
+        slb[hf] = sl
+        sall[hf * hrows:(hf + 1) * hrows] = spread(sl, b_of - first, hblk)
+
+    def query_terms(hf):
+        dq_part = mm(spread(slb[hf], meta[hf * hrows:(hf + 1) * hrows, 0:1], nblk), w_ref[...])
+        sbuf2[hf * LIST:(hf + 1) * LIST] = dq_part.reshape(LIST, cap, dim).astype(BF16)
+
+    def partner_rows(hf):
+        at_row = slots + hf * hrows
+        fwd_rows(hf).wait_recv()
+        x = xall[at_row:at_row + hrows]
+        b_of = meta_x[hf * hrows:(hf + 1) * hrows, 0:1] - first
+        w_half = w_ref[pl.ds(pl.multiple_of(core * half, half), half), :]
+        sl = slope128(x, w_half, b_of, meta_x[hf * hrows:(hf + 1) * hrows, 1:2], hblk)
+        sall[at_row:at_row + hrows] = spread(sl, b_of, hblk)
+
+    load_w.wait()
+    bulk(rbuf.at[pl.ds(0, N_NEAR - 1)], rnear).wait_recv()
+    own_rows(0)
+    fwd_meta.wait_recv()
+    partner_rows(0)
+    query_terms(0)
+    bulk(rbuf.at[pl.ds(LIST, LIST)], rfar).wait_recv()
+    for dz, dy in near:
+        remote(sbuf2.at[2 * (dz + HOP - 1) + dy], nbuf.at[2 * (HOP - 1 - dz) + dy], s2, rn, (p, at(dy, dz))).start()
+    nbuf[SELF_NEAR:SELF_NEAR + 1] = sbuf2[SELF_NEAR:SELF_NEAR + 1]
+    own_rows(1)
+    query_terms(1)
     for s in range(2):
         for jj in range(N_RELAY - 1, 0, -1):
             dy, dz = stop(s, jj)
-            relay_dz = -dz
-            home = at(dy, relay_dz - HOP if s == 0 else relay_dz + HOP)
-            remote(sbuf2.at[home], rrbuf.at[s, jj], s2, rr.at[s], (p, at(dy, relay_dz))).start()
-        rrbuf[s, 0:1] = sbuf2[pl.ds(srcs[s], 1)]
-    for dz, dy in near:
-        home = at(dy, dz)
-        remote(sbuf2.at[home], nbuf.at[2 * (HOP - 1 - dz) + dy], s2, rn, (p, home)).start()
-    nbuf[SELF_NEAR:SELF_NEAR + 1] = sbuf2[pl.ds(me, 1)]
-
-    hblk = nblk // 2
-    first = core.astype(F32) * hblk
-    dw = mm(spread(sl, blk_s - first, hblk), x, 0, 0)
-    fwd_meta.wait_recv()
-    fwd_rows.wait_recv()
-    x2 = xbuf[...].astype(F32).reshape(slots, dim).astype(BF16)
-    m2 = meta_x[...]
-    b2 = m2[:, 0:1] - first
-    w_half = w_ref[pl.ds(pl.multiple_of(core * half, half), half), :]
-    sl2 = slope128(x2, w_half, b2, m2[:, 1:2], hblk)
-    dw = dw + mm(spread(sl2, b2, hblk), x2, 0, 0)
-    dwbuf[...] = dw.astype(BF16).reshape(chips, piece, dim)
-    for t in range(1, chips):
-        to = lax.rem(chip + t, chips)
-        remote(dwbuf.at[to], dwrecv.at[chip], s3, r3, (2 * to + core, me)).start()
-    dwrecv[pl.ds(chip, 1)] = dwbuf[pl.ds(chip, 1)]
+            remote(sbuf2.at[far_slot(s, jj)], rrbuf.at[s, jj], s2, rr.at[s], (p, at(dy, -dz))).start()
+        rrbuf[s, 0:1] = sbuf2[N_NEAR + s:N_NEAR + s + 1]
+    partner_rows(1)
+
+    nx = chips // 2
+    chip_h, chip_x = lax.div(chip, nx), lax.rem(chip, nx)
+
+    def chip_at(dh, dx):
+        return lax.rem(chip_h + dh, 2) * nx + lax.rem(chip_x + dx + nx, nx)
+
+    others = [(1, dx) for dx in range(nx - 1, -1, -1)] + [(0, dx) for dx in range(nx - 1, 0, -1)]
+    for g in range(PARTS):
+        dw = mm(sall[:, g * part:(g + 1) * part], xall[...], 0, 0)
+        dwbuf[g] = dw.astype(BF16).reshape(chips, piece, dim)
+        for dh, dx in others:
+            to = chip_at(dh, dx)
+            remote(dwbuf.at[g, to], dwrecv.at[g, chip], s3.at[g], r3.at[g], (2 * to + core, me)).start()
+        dwrecv[g, pl.ds(chip, 1)] = dwbuf[g, pl.ds(chip, 1)]
 
     def to_home(s):
         return remote(fsend.at[s], fback.at[s], sb.at[s], rb.at[s], (p, srcs[s]))
@@ -221,38 +256,53 @@
         fsend[s] = mm(prel[s * width:(s + 1) * width], terms, 0, 0).astype(BF16)
         to_home(s).start()
 
-    bulk(dwrecv.at[pl.ds(0, chips - 1)], r3).wait_recv()
-    total = dwrecv[0].astype(F32)
-    for j in range(1, chips):
-        total = total + dwrecv[j].astype(F32)
-    done = (total / n_pb).astype(BF16)
-    fin[...] = done
-
-    def rows_of(c_, j):
-        return pl.ds(pl.multiple_of(c_ * half + j * piece, piece), piece)
-
-    wg_ref[rows_of(core, chip), :] = done
-
-    def share(to, j):
-        return remote(fin, wg_ref.at[rows_of(core, j)], s4, r4.at[j], (2 * to + core, me))
-
-    for t in range(1, chips):
-        share(lax.rem(chip + t, chips), chip).start()
-    remote(fin, wg_ref.at[rows_of(core, chip)], s5, r5, (partner, me)).start()
-
-    bulk(nbuf.at[pl.ds(0, N_NEAR - 1)], rn).wait_recv()
-    terms = nbuf[...].astype(F32).reshape(width, dim).astype(BF16)
-    home_sum = mm(pown[...], terms, 0, 0)
-    for s in range(2):
-        to_home(s).wait_recv()
-        home_sum = home_sum + fback[s].astype(F32)
-    dq_ref[...] = home_sum
-
-    for t in range(1, chips):
-        other = lax.rem(chip + t, chips)
-        share(other, other).wait_recv()
-        there = wg_ref.at[rows_of(core, other)]
+    def rows_of(c_, g, j):
+        return pl.ds(pl.multiple_of(c_ * half + g * part + j * piece, piece), piece)
+
+    def share(g, to, j):
+        return remote(fin.at[g], wg_ref.at[rows_of(core, g, j)], s4.at[g], r4.at[g, j], (2 * to + core, me))
+
+    ring = nx > 2
+    direct = [(1, 0)] + ([(0, 2), (0, 1), (0, -1)] if ring else [(0, dx) for dx in range(1, nx)])
+    passed = {(1, 0): [(0, 1), (0, -1)] if ring else [(0, dx) for dx in range(1, nx)], (0, 2): [(1, 0)]}
+    second = [(1, 1), (1, -1), (1, 2)] if ring else [(1, dx) for dx in range(1, nx)]
+
+    for g in range(PARTS):
+        bulk(dwrecv.at[g, pl.ds(0, chips - 1)], r3.at[g]).wait_recv()
+        total = dwrecv[g, 0].astype(F32)
+        for j in range(1, chips):
+            total = total + dwrecv[g, j].astype(F32)
+        done = (total / n_pb).astype(BF16)
+        fin[g] = done
+        wg_ref[rows_of(core, g, chip), :] = done
+        for dh, dx in direct:
+            share(g, chip_at(dh, dx), chip).start()
+        remote(fin.at[g], wg_ref.at[rows_of(core, g, chip)], s5, r5, (partner, me)).start()
+
+    def query_home():
+        bulk(nbuf.at[pl.ds(0, N_NEAR - 1)], rn).wait_recv()
+        terms = nbuf[...].astype(F32).reshape(width, dim).astype(BF16)
+        home_sum = mm(pown[...], terms, 0, 0)
+        for s in range(2):
+            to_home(s).wait_recv()
+            home_sum = home_sum + fback[s].astype(F32)
+        dq_ref[...] = home_sum
+
+    def arrived(g, dh, dx):
+        owner = chip_at(dh, dx)
+        share(g, owner, owner).wait_recv()
+        there = wg_ref.at[rows_of(core, g, owner)]
+        for fh, fx in passed.get((dh, dx), []):
+            remote(there, there, s4.at[g], r4.at[g, owner], (2 * chip_at(fh, fx) + core, me)).start()
         remote(there, there, s5, r5, (partner, me)).start()
+
+    for g in range(PARTS):
+        for dh, dx in direct:
+            arrived(g, dh, dx)
+    query_home()
+    for g in range(PARTS):
+        for dh, dx in second:
+            arrived(g, dh, dx)
     bulk(wg_ref.at[pl.ds(pl.multiple_of((1 - core) * half, half), half)], r5).wait_recv()
 
     bulk(sbuf.at[pl.ds(0, N_NEAR - 1)], s1.at[0]).wait_send()
@@ -260,11 +310,12 @@
         chunk_out(s).wait_send()
         bulk(relbuf.at[s, pl.ds(0, N_RELAY - 1)], sr.at[s]).wait_send()
         to_home(s).wait_send()
+        fwd_rows(s).wait_send()
     fwd_meta.wait_send()
-    fwd_rows.wait_send()
-    bulk(sbuf2.at[pl.ds(0, n_in)], s2).wait_send()
-    bulk(dwbuf.at[pl.ds(0, chips - 1)], s3).wait_send()
-    bulk(dwbuf.at[pl.ds(0, chips - 1)], s4).wait_send()
+    bulk(sbuf2.at[pl.ds(0, n_lab - 3)], s2).wait_send()
+    for g in range(PARTS):
+        bulk(dwbuf.at[g, pl.ds(0, chips - 1)], s3.at[g]).wait_send()
+        bulk(dwbuf.at[g, pl.ds(0, chips - 1)], s4.at[g]).wait_send()
     bulk(wg_ref.at[pl.ds(pl.multiple_of(core * half, half), half)], s5).wait_send()
 
 
@@ -284,7 +335,7 @@
     cap = rows * kk // n_lab
     slots = n_lab * cap
     chips = n_pb // 2
-    piece = labels // 2 // chips
+    piece = labels // 2 // PARTS // chips
     width = LIST * cap
     sib = sibling_blocks.T
     pos = positive_slot.reshape(1, -1)
@@ -301,13 +352,14 @@
         in_specs=[vmem, hbm, vmem, vmem],
         out_specs=(vmem, vmem),
         scratch_shapes=[
-            buf(labels), buf(LIST, cap), buf(2, rows), buf(2, LIST, cap), buf(n_lab, cap), buf(n_lab, cap),
+            buf(labels), buf(LIST, cap), buf(2, rows), buf(2, LIST, cap), buf(n_lab, cap), buf(2 * slots),
+            pltpu.VMEM((2 * slots, labels // 2), BF16), pltpu.VMEM((2, slots // 2, BLOCK), F32),
             pltpu.VMEM((width, rows), BF16), pltpu.VMEM((2 * width, rows), BF16),
             pltpu.VMEM((slots, BLOCK), F32), pltpu.VMEM((slots, BLOCK), F32),
             buf(n_lab, cap), buf(LIST, cap), buf(2, LIST, cap), buf(2, rows), buf(2, rows),
-            buf(chips, piece), buf(chips, piece), buf(piece),
-            dma, dma((1,)), dma, dma((2,)), dma((2,)), dma((2,)), dma((2,)), dma((2,)), dma, dma, dma((2,)), dma((2,)), dma((2,)),
-            dma, dma, dma, dma((chips,)), dma, dma,
+            buf(PARTS, chips, piece), buf(PARTS, chips, piece), buf(PARTS, piece),
+            dma, dma((1,)), dma, dma, dma((2,)), dma((2,)), dma((2,)), dma((3,)), dma((3,)), dma, dma, dma((2,)), dma((2,)), dma((2,)),
+            dma((PARTS,)), dma((PARTS,)), dma((PARTS,)), dma((PARTS, chips)), dma, dma,
         ],
         compiler_params=pltpu.CompilerParams(collective_id=0, has_side_effects=True),
     )(queries, label_weights, sib, pos)

time: 63.2 us -> 58.4 us (0.924)
  Pallas kernels: 62.4 us -> 57.6 us
    pallas_call x1, Pallas kernels: 61.2 us -> 56.4 us  [shards(): pl.pallas_call(functools.partial(kernel, n_pb, n_lab), out_shape=(pltpu.V...]
where the time goes in v3:
time: 58.4 us; the launch traced here: 58.2 us
  Pallas kernels  57.6 us (99%)
  between operations  0.64 us (1%)
    pallas_call x1, Pallas kernels, shards(): pl.pallas_call(functools.partial(kernel, n_pb, n_lab), out_shape=(pltpu.V...  56.4 us
    pallas_call x1, Pallas kernels, shards(): pl.pallas_call(write_out, out_shape=(jax.ShapeDtypeStruct((rows, dim), F3...  1.18 us

profile of v3, /device:TPU:1, one launch (start us, length us, event | category | flops | bytes accessed | tf_op | source)
XLA Modules:
  0.0 58.2 jit_solution(16862515521105389367)
XLA Ops:
  0.6 56.4 %shard_map.59 = (f32[32,768]{1,0:T(8,128)S(1)}, bf16[1024,768]{1,0:T(8,128)(2,1)S(1)}) custom-call(bf16[32,768]{1,0:T(8,128)(2,1)} %q_ref.1, bf16[1024,768]{1,0:T(8,128)(2,1)} %w_hbm.1, s32[8,1024]{1,0:T(8,128)} %bitcast.2, s32[1,1024]{1,0:T(1,128)} %bitcast.3), custom_call_target="tpu_custom_call" | custom-call | tf_op jit(solution)/shard_map/pallas_call | solution.py:349
  57.1 1.2 %shard_map.60 = (f32[32,768]{1,0:T(8,128)}, bf16[1024,768]{1,0:T(8,128)(2,1)}) custom-call(f32[32,768]{1,0:T(8,128)S(1)} %get-tuple-element.4.a_ref, bf16[1024,768]{1,0:T(8,128)(2,1)S(1)} %get-tuple-element.5.b_ref), custom_call_target="tpu_custom_call" | custom-call | tf_op jit(solution)/shard_map/pallas_call | solution.py:367

commit v4 on v3

--- a/solution.py
+++ b/solution.py
@@ -27,11 +27,11 @@
     return lax.broadcasted_iota(jnp.int32, shape, ax)
 
 
-def kernel(n_pb, n_lab, q_ref, w_hbm, sib_ref, pos_ref, dq_ref, wg_ref, w_ref, sbuf, fbuf, relbuf, rbuf, xall, sall, slb, pown, prel, meta, meta_x,
-           sbuf2, nbuf, rrbuf, fsend, fback, dwbuf, dwrecv, fin,
-           sw, s1, rnear, rfar, sf, rf, sr, sx, rx, s2, rn, rr, sb, rb, s3, r3, s4, r4, s5, r5):
-    kk, total_rows = sib_ref.shape
-    rows, dim = q_ref.shape
+def kernel(n_pb, n_lab, q_hbm, w_hbm, sib_hbm, pos_hbm, dq_ref, wg_ref, q_ref, sib_ref, pos_ref, w_ref, sbuf, fbuf, relbuf, rbuf, xall, sall, slb, pown, prel, meta, meta_x,
+           sbuf2, nbuf, rrbuf, fsend, fback, dwbuf, dwrecv, comb, fin,
+           sq, sw, s1, rnear, rfar, sf, rf, sr, sx, rx, s2, rn, rr, sb, rb, s3, r3, s4, r4, s5, r5, r6):
+    kk, total_rows = sib_hbm.shape
+    rows, dim = q_hbm.shape
     cap = rows * kk // n_lab
     slots = n_lab * cap
     labels = w_hbm.shape[0]
@@ -52,6 +52,12 @@
     def at(dy, dz):
         return lax.rem(my_y + dy, 2) * nz + lax.rem(my_z + dz + nz, nz)
 
+    loads = [
+        pltpu.make_async_copy(src, dst, sq.at[n])
+        for n, (src, dst) in enumerate(((sib_hbm, sib_ref), (q_hbm, q_ref), (pos_hbm, pos_ref)))
+    ]
+    for load in loads:
+        load.start()
     load_w = pltpu.make_async_copy(w_hbm, w_ref, sw)
     load_w.start()
 
@@ -73,6 +79,8 @@
         on = mm(expand, hit_b)
         return jnp.logical_and(on > 0.5, mm(expand, rank.astype(BF16)) == want)
 
+    for load in loads:
+        load.wait()
     sib = sib_ref[...]
     col = iota((total_rows, 3 * rows), 1)
     run_of = jnp.where(col < rows, me, jnp.where(col < 2 * rows, src_a, src_b))
@@ -238,46 +246,64 @@
     def chip_at(dh, dx):
         return lax.rem(chip_h + dh, 2) * nx + lax.rem(chip_x + dx + nx, nx)
 
-    others = [(1, dx) for dx in range(nx - 1, -1, -1)] + [(0, dx) for dx in range(nx - 1, 0, -1)]
+    ring = nx > 2
+    others = [(1, 1), (1, -1), (0, 2), (0, 1), (0, -1)] if ring else [(1, dx) for dx in range(nx)] + [(0, dx) for dx in range(1, nx)]
+    across = chip_at(1, 0)
+
+    def to_across(g):
+        return remote(dwbuf.at[g, across], dwrecv.at[g, chip], s3.at[g], r3.at[g], (2 * across + core, me))
+
+    def corner(g):
+        return remote(dwbuf.at[g, chip_at(1, 2)], comb.at[g], s3.at[g], r6.at[g], (2 * chip_at(0, 2) + core, me))
+
     for g in range(PARTS):
         dw = mm(sall[:, g * part:(g + 1) * part], xall[...], 0, 0)
         dwbuf[g] = dw.astype(BF16).reshape(chips, piece, dim)
+        if ring:
+            corner(g).start()
         for dh, dx in others:
             to = chip_at(dh, dx)
             remote(dwbuf.at[g, to], dwrecv.at[g, chip], s3.at[g], r3.at[g], (2 * to + core, me)).start()
         dwrecv[g, pl.ds(chip, 1)] = dwbuf[g, pl.ds(chip, 1)]
 
+    if ring:
+        for g in range(PARTS):
+            corner(g).wait_recv()
+            both = dwbuf[g, pl.ds(across, 1)].astype(F32) + comb[g:g + 1].astype(F32)
+            dwbuf[g, pl.ds(across, 1)] = both.astype(BF16)
+            to_across(g).start()
+
     def to_home(s):
         return remote(fsend.at[s], fback.at[s], sb.at[s], rb.at[s], (p, srcs[s]))
 
-    for s in range(2):
-        bulk(rrbuf.at[s, pl.ds(0, N_RELAY - 1)], rr.at[s]).wait_recv()
-        terms = rrbuf[s].astype(F32).reshape(width, dim).astype(BF16)
-        fsend[s] = mm(prel[s * width:(s + 1) * width], terms, 0, 0).astype(BF16)
-        to_home(s).start()
-
     def rows_of(c_, g, j):
         return pl.ds(pl.multiple_of(c_ * half + g * part + j * piece, piece), piece)
 
     def share(g, to, j):
         return remote(fin.at[g], wg_ref.at[rows_of(core, g, j)], s4.at[g], r4.at[g, j], (2 * to + core, me))
 
-    ring = nx > 2
     direct = [(1, 0)] + ([(0, 2), (0, 1), (0, -1)] if ring else [(0, dx) for dx in range(1, nx)])
     passed = {(1, 0): [(0, 1), (0, -1)] if ring else [(0, dx) for dx in range(1, nx)], (0, 2): [(1, 0)]}
     second = [(1, 1), (1, -1), (1, 2)] if ring else [(1, dx) for dx in range(1, nx)]
 
     for g in range(PARTS):
-        bulk(dwrecv.at[g, pl.ds(0, chips - 1)], r3.at[g]).wait_recv()
-        total = dwrecv[g, 0].astype(F32)
-        for j in range(1, chips):
-            total = total + dwrecv[g, j].astype(F32)
-        done = (total / n_pb).astype(BF16)
+        came = others + ([(1, 0)] if ring else [])
+        bulk(dwrecv.at[g, pl.ds(0, len(came))], r3.at[g]).wait_recv()
+        total = dwrecv[g, pl.ds(chip, 1)].astype(F32)
+        for dh, dx in came:
+            total = total + dwrecv[g, pl.ds(chip_at(dh, dx), 1)].astype(F32)
+        done = (total[0] / n_pb).astype(BF16)
         fin[g] = done
         wg_ref[rows_of(core, g, chip), :] = done
         for dh, dx in direct:
             share(g, chip_at(dh, dx), chip).start()
         remote(fin.at[g], wg_ref.at[rows_of(core, g, chip)], s5, r5, (partner, me)).start()
+        if g == 0:
+            for s in range(2):
+                bulk(rrbuf.at[s, pl.ds(0, N_RELAY - 1)], rr.at[s]).wait_recv()
+                terms = rrbuf[s].astype(F32).reshape(width, dim).astype(BF16)
+                fsend[s] = mm(prel[s * width:(s + 1) * width], terms, 0, 0).astype(BF16)
+                to_home(s).start()
 
     def query_home():
         bulk(nbuf.at[pl.ds(0, N_NEAR - 1)], rn).wait_recv()
@@ -299,10 +325,10 @@
     for g in range(PARTS):
         for dh, dx in direct:
             arrived(g, dh, dx)
-    query_home()
     for g in range(PARTS):
         for dh, dx in second:
             arrived(g, dh, dx)
+    query_home()
     bulk(wg_ref.at[pl.ds(pl.multiple_of((1 - core) * half, half), half)], r5).wait_recv()
 
     bulk(sbuf.at[pl.ds(0, N_NEAR - 1)], s1.at[0]).wait_send()
@@ -349,17 +375,18 @@
     dq, wg = pl.pallas_call(
         functools.partial(kernel, n_pb, n_lab),
         out_shape=(pltpu.VMEM((rows, dim), F32), pltpu.VMEM((labels, dim), BF16)),
-        in_specs=[vmem, hbm, vmem, vmem],
+        in_specs=[hbm] * 4,
         out_specs=(vmem, vmem),
         scratch_shapes=[
+            buf(rows), pltpu.VMEM(sib.shape, jnp.int32), pltpu.VMEM(pos.shape, jnp.int32),
             buf(labels), buf(LIST, cap), buf(2, rows), buf(2, LIST, cap), buf(n_lab, cap), buf(2 * slots),
             pltpu.VMEM((2 * slots, labels // 2), BF16), pltpu.VMEM((2, slots // 2, BLOCK), F32),
             pltpu.VMEM((width, rows), BF16), pltpu.VMEM((2 * width, rows), BF16),
             pltpu.VMEM((slots, BLOCK), F32), pltpu.VMEM((slots, BLOCK), F32),
             buf(n_lab, cap), buf(LIST, cap), buf(2, LIST, cap), buf(2, rows), buf(2, rows),
-            buf(PARTS, chips, piece), buf(PARTS, chips, piece), buf(PARTS, piece),
-            dma, dma((1,)), dma, dma, dma((2,)), dma((2,)), dma((2,)), dma((3,)), dma((3,)), dma, dma, dma((2,)), dma((2,)), dma((2,)),
-            dma((PARTS,)), dma((PARTS,)), dma((PARTS,)), dma((PARTS, chips)), dma, dma,
+            buf(PARTS, chips, piece), buf(PARTS, chips, piece), buf(PARTS, piece), buf(PARTS, piece),
+            dma((3,)), dma, dma((1,)), dma, dma, dma((2,)), dma((2,)), dma((2,)), dma((3,)), dma((3,)), dma, dma, dma((2,)), dma((2,)), dma((2,)),
+            dma((PARTS,)), dma((PARTS,)), dma((PARTS,)), dma((PARTS, chips)), dma, dma, dma((PARTS,)),
         ],
         compiler_params=pltpu.CompilerParams(collective_id=0, has_side_effects=True),
     )(queries, label_weights, sib, pos)

time: 58.4 us -> 56.3 us (0.964)
  Pallas kernels: 57.6 us -> 55.5 us
    pallas_call x1, Pallas kernels: 56.4 us -> 54.3 us  [shards(): pl.pallas_call(functools.partial(kernel, n_pb, n_lab), out_shape=(pltpu.V...]
where the time goes in v4:
time: 56.3 us; the launch traced here: 56.1 us
  Pallas kernels  55.5 us (99%)
  between operations  0.64 us (1%)
    pallas_call x1, Pallas kernels, shards(): pl.pallas_call(functools.partial(kernel, n_pb, n_lab), out_shape=(pltpu.V...  54.3 us
    pallas_call x1, Pallas kernels, shards(): pl.pallas_call(write_out, out_shape=(jax.ShapeDtypeStruct((rows, dim), F3...  1.18 us

profile of v4, /device:TPU:1, one launch (start us, length us, event | category | flops | bytes accessed | tf_op | source)
XLA Modules:
  0.0 56.1 jit_solution(15278992625057089893)
XLA Ops:
  0.6 54.3 %shard_map.59 = (f32[32,768]{1,0:T(8,128)S(1)}, bf16[1024,768]{1,0:T(8,128)(2,1)S(1)}) custom-call(bf16[32,768]{1,0:T(8,128)(2,1)} %q_hbm.1, bf16[1024,768]{1,0:T(8,128)(2,1)} %w_hbm.1, s32[8,1024]{1,0:T(8,128)} %bitcast.2, s32[1,1024]{1,0:T(1,128)} %bitcast.3), custom_call_target="tpu_custom_call" | custom-call | tf_op jit(solution)/shard_map/pallas_call | solution.py:375
  54.9 1.2 %shard_map.60 = (f32[32,768]{1,0:T(8,128)}, bf16[1024,768]{1,0:T(8,128)(2,1)}) custom-call(f32[32,768]{1,0:T(8,128)S(1)} %get-tuple-element.4.a_ref, bf16[1024,768]{1,0:T(8,128)(2,1)S(1)} %get-tuple-element.5.b_ref), custom_call_target="tpu_custom_call" | custom-call | tf_op jit(solution)/shard_map/pallas_call | solution.py:394

commit v5 on v4

--- a/solution.py
+++ b/solution.py
@@ -62,8 +62,8 @@
     load_w.start()
 
     barrier = pltpu.get_barrier_semaphore()
-    for dz in range(-HOP, HOP + 1):
-        for dy in range(2):
+    for dz in sorted(range(-HOP, HOP + 1), key=abs, reverse=True):
+        for dy in (1, 0):
             if dz or dy:
                 pl.semaphore_signal(barrier, inc=1, device_id=(p, at(dy, dz)), device_id_type=MESH)
     pl.semaphore_signal(barrier, inc=1, device_id=(partner, me), device_id_type=MESH)
@@ -124,10 +124,6 @@
     chunk_out(0).start()
     chunk_out(1).start()
     near = [(dz * sg, dy) for dz in range(HOP - 1, -1, -1) for sg in ((1, -1) if dz else (1,)) for dy in (0, 1) if dz or dy]
-    for dz, dy in near:
-        j = 2 * (dz + HOP - 1) + dy
-        remote(sbuf.at[j], rbuf.at[2 * (HOP - 1 - dz) + dy], s1.at[0], rnear, (p, at(dy, dz))).start()
-    rbuf[SELF_NEAR:SELF_NEAR + 1] = sbuf[SELF_NEAR:SELF_NEAR + 1]
 
     qrow = iota((n_lab, total_rows), 1)
     in_run = jnp.right_shift(qrow, 5) == iota((n_lab, total_rows), 0)
@@ -155,6 +151,10 @@
     meta[...] = jnp.where(lane == 0, blk_s, pc_s)
     fwd_meta = remote(meta, meta_x, sx.at[0], rx.at[0], (partner, me))
     fwd_meta.start()
+    for dz, dy in near:
+        j = 2 * (dz + HOP - 1) + dy
+        remote(sbuf.at[j], rbuf.at[2 * (HOP - 1 - dz) + dy], s1.at[0], rnear, (p, at(dy, dz))).start()
+    rbuf[SELF_NEAR:SELF_NEAR + 1] = sbuf[SELF_NEAR:SELF_NEAR + 1]
     nbuf[N_NEAR:] = jnp.zeros((LIST - N_NEAR, cap, dim), BF16)
     rrbuf[0, N_RELAY:] = jnp.zeros((LIST - N_RELAY, cap, dim), BF16)
     rrbuf[1, N_RELAY:] = jnp.zeros((LIST - N_RELAY, cap, dim), BF16)
@@ -199,10 +199,17 @@
     def fwd_rows(hf):
         return remote(xall.at[pl.ds(hf * hrows, hrows)], xall.at[pl.ds(slots + hf * hrows, hrows)], sx.at[1 + hf], rx.at[1 + hf], (partner, me))
 
+    def near_home():
+        for dz, dy in near:
+            remote(sbuf2.at[2 * (dz + HOP - 1) + dy], nbuf.at[2 * (HOP - 1 - dz) + dy], s2, rn, (p, at(dy, dz))).start()
+        nbuf[SELF_NEAR:SELF_NEAR + 1] = sbuf2[SELF_NEAR:SELF_NEAR + 1]
+
     def own_rows(hf):
         x = rbuf[hf * LIST:(hf + 1) * LIST].astype(F32).reshape(hrows, dim).astype(BF16)
         xall[hf * hrows:(hf + 1) * hrows] = x
         fwd_rows(hf).start()
+        if hf:
+            near_home()
         b_of = meta[hf * hrows:(hf + 1) * hrows, 0:1]
         sl = slope128(x, w_ref[...], b_of, meta[hf * hrows:(hf + 1) * hrows, 1:2], nblk)
         slb[hf] = sl
@@ -228,9 +235,6 @@
     partner_rows(0)
     query_terms(0)
     bulk(rbuf.at[pl.ds(LIST, LIST)], rfar).wait_recv()
-    for dz, dy in near:
-        remote(sbuf2.at[2 * (dz + HOP - 1) + dy], nbuf.at[2 * (HOP - 1 - dz) + dy], s2, rn, (p, at(dy, dz))).start()
-    nbuf[SELF_NEAR:SELF_NEAR + 1] = sbuf2[SELF_NEAR:SELF_NEAR + 1]
     own_rows(1)
     query_terms(1)
     for s in range(2):

time: 56.3 us -> 56.3 us (level)
  no operation moved by 1% of the time
where the time goes in v5:
time: 56.3 us; the launch traced here: 56.2 us
  Pallas kernels  55.5 us (99%)
  between operations  0.64 us (1%)
    pallas_call x1, Pallas kernels, shards(): pl.pallas_call(functools.partial(kernel, n_pb, n_lab), out_shape=(pltpu.V...  54.4 us
    pallas_call x1, Pallas kernels, shards(): pl.pallas_call(write_out, out_shape=(jax.ShapeDtypeStruct((rows, dim), F3...  1.18 us

profile of v5, /device:TPU:1, one launch (start us, length us, event | category | flops | bytes accessed | tf_op | source)
XLA Modules:
  0.0 56.2 jit_solution(13639125817692578940)
XLA Ops:
  0.6 54.4 %shard_map.59 = (f32[32,768]{1,0:T(8,128)S(1)}, bf16[1024,768]{1,0:T(8,128)(2,1)S(1)}) custom-call(bf16[32,768]{1,0:T(8,128)(2,1)} %q_hbm.1, bf16[1024,768]{1,0:T(8,128)(2,1)} %w_hbm.1, s32[8,1024]{1,0:T(8,128)} %bitcast.2, s32[1,1024]{1,0:T(1,128)} %bitcast.3), custom_call_target="tpu_custom_call" | custom-call | tf_op jit(solution)/shard_map/pallas_call | solution.py:379
  55.0 1.2 %shard_map.60 = (f32[32,768]{1,0:T(8,128)}, bf16[1024,768]{1,0:T(8,128)(2,1)}) custom-call(f32[32,768]{1,0:T(8,128)S(1)} %get-tuple-element.4.a_ref, bf16[1024,768]{1,0:T(8,128)(2,1)S(1)} %get-tuple-element.5.b_ref), custom_call_target="tpu_custom_call" | custom-call | tf_op jit(solution)/shard_map/pallas_call | solution.py:398

commit v6 on v5

--- a/solution.py
+++ b/solution.py
@@ -28,7 +28,7 @@
 
 
 def kernel(n_pb, n_lab, q_hbm, w_hbm, sib_hbm, pos_hbm, dq_ref, wg_ref, q_ref, sib_ref, pos_ref, w_ref, sbuf, fbuf, relbuf, rbuf, xall, sall, slb, pown, prel, meta, meta_x,
-           sbuf2, nbuf, rrbuf, fsend, fback, dwbuf, dwrecv, comb, fin,
+           sbuf2, nbuf, rrbuf, fsend, fback, dwbuf, dwrecv, comb, fin, dwacc,
            sq, sw, s1, rnear, rfar, sf, rf, sr, sx, rx, s2, rn, rr, sb, rb, s3, r3, s4, r4, s5, r5, r6):
     kk, total_rows = sib_hbm.shape
     rows, dim = q_hbm.shape
@@ -197,7 +197,7 @@
         return jnp.concatenate([jnp.where(b_of == float(b), sl, 0.0) for b in range(n)], axis=1).astype(BF16)
 
     def fwd_rows(hf):
-        return remote(xall.at[pl.ds(hf * hrows, hrows)], xall.at[pl.ds(slots + hf * hrows, hrows)], sx.at[1 + hf], rx.at[1 + hf], (partner, me))
+        return remote(xall.at[pl.ds(2 * hf * hrows, hrows)], xall.at[pl.ds((2 * hf + 1) * hrows, hrows)], sx.at[1 + hf], rx.at[1 + hf], (partner, me))
 
     def near_home():
         for dz, dy in near:
@@ -206,21 +206,21 @@
 
     def own_rows(hf):
         x = rbuf[hf * LIST:(hf + 1) * LIST].astype(F32).reshape(hrows, dim).astype(BF16)
-        xall[hf * hrows:(hf + 1) * hrows] = x
+        xall[2 * hf * hrows:(2 * hf + 1) * hrows] = x
         fwd_rows(hf).start()
         if hf:
             near_home()
         b_of = meta[hf * hrows:(hf + 1) * hrows, 0:1]
         sl = slope128(x, w_ref[...], b_of, meta[hf * hrows:(hf + 1) * hrows, 1:2], nblk)
         slb[hf] = sl
-        sall[hf * hrows:(hf + 1) * hrows] = spread(sl, b_of - first, hblk)
+        sall[2 * hf * hrows:(2 * hf + 1) * hrows] = spread(sl, b_of - first, hblk)
 
     def query_terms(hf):
         dq_part = mm(spread(slb[hf], meta[hf * hrows:(hf + 1) * hrows, 0:1], nblk), w_ref[...])
         sbuf2[hf * LIST:(hf + 1) * LIST] = dq_part.reshape(LIST, cap, dim).astype(BF16)
 
     def partner_rows(hf):
-        at_row = slots + hf * hrows
+        at_row = (2 * hf + 1) * hrows
         fwd_rows(hf).wait_recv()
         x = xall[at_row:at_row + hrows]
         b_of = meta_x[hf * hrows:(hf + 1) * hrows, 0:1] - first
@@ -234,6 +234,8 @@
     fwd_meta.wait_recv()
     partner_rows(0)
     query_terms(0)
+    for g in range(PARTS):
+        dwacc[g] = mm(sall[:slots, g * part:(g + 1) * part], xall[:slots], 0, 0)
     bulk(rbuf.at[pl.ds(LIST, LIST)], rfar).wait_recv()
     own_rows(1)
     query_terms(1)
@@ -261,7 +263,7 @@
         return remote(dwbuf.at[g, chip_at(1, 2)], comb.at[g], s3.at[g], r6.at[g], (2 * chip_at(0, 2) + core, me))
 
     for g in range(PARTS):
-        dw = mm(sall[:, g * part:(g + 1) * part], xall[...], 0, 0)
+        dw = dwacc[g] + mm(sall[slots:, g * part:(g + 1) * part], xall[slots:], 0, 0)
         dwbuf[g] = dw.astype(BF16).reshape(chips, piece, dim)
         if ring:
             corner(g).start()
@@ -302,7 +304,7 @@
         for dh, dx in direct:
             share(g, chip_at(dh, dx), chip).start()
         remote(fin.at[g], wg_ref.at[rows_of(core, g, chip)], s5, r5, (partner, me)).start()
-        if g == 0:
+        if g == PARTS - 1:
             for s in range(2):
                 bulk(rrbuf.at[s, pl.ds(0, N_RELAY - 1)], rr.at[s]).wait_recv()
                 terms = rrbuf[s].astype(F32).reshape(width, dim).astype(BF16)
@@ -389,6 +391,7 @@
             pltpu.VMEM((slots, BLOCK), F32), pltpu.VMEM((slots, BLOCK), F32),
             buf(n_lab, cap), buf(LIST, cap), buf(2, LIST, cap), buf(2, rows), buf(2, rows),
             buf(PARTS, chips, piece), buf(PARTS, chips, piece), buf(PARTS, piece), buf(PARTS, piece),
+            pltpu.VMEM((PARTS, labels // 2 // PARTS, dim), F32),
             dma((3,)), dma, dma((1,)), dma, dma, dma((2,)), dma((2,)), dma((2,)), dma((3,)), dma((3,)), dma, dma, dma((2,)), dma((2,)), dma((2,)),
             dma((PARTS,)), dma((PARTS,)), dma((PARTS,)), dma((PARTS, chips)), dma, dma, dma((PARTS,)),
         ],

time: 56.3 us -> 56.2 us (level)
  no operation moved by 1% of the time
where the time goes in v6:
time: 56.2 us; the launch traced here: 56.1 us
  Pallas kernels  55.4 us (99%)
  between operations  0.64 us (1%)
    pallas_call x1, Pallas kernels, shards(): pl.pallas_call(functools.partial(kernel, n_pb, n_lab), out_shape=(pltpu.V...  54.3 us
    pallas_call x1, Pallas kernels, shards(): pl.pallas_call(write_out, out_shape=(jax.ShapeDtypeStruct((rows, dim), F3...  1.18 us

profile of v6, /device:TPU:1, one launch (start us, length us, event | category | flops | bytes accessed | tf_op | source)
XLA Modules:
  0.0 56.1 jit_solution(7717392552368687362)
XLA Ops:
  0.6 54.3 %shard_map.59 = (f32[32,768]{1,0:T(8,128)S(1)}, bf16[1024,768]{1,0:T(8,128)(2,1)S(1)}) custom-call(bf16[32,768]{1,0:T(8,128)(2,1)} %q_hbm.1, bf16[1024,768]{1,0:T(8,128)(2,1)} %w_hbm.1, s32[8,1024]{1,0:T(8,128)} %bitcast.2, s32[1,1024]{1,0:T(1,128)} %bitcast.3), custom_call_target="tpu_custom_call" | custom-call | tf_op jit(solution)/shard_map/pallas_call | solution.py:381
  54.9 1.2 %shard_map.60 = (f32[32,768]{1,0:T(8,128)}, bf16[1024,768]{1,0:T(8,128)(2,1)}) custom-call(f32[32,768]{1,0:T(8,128)S(1)} %get-tuple-element.4.a_ref, bf16[1024,768]{1,0:T(8,128)(2,1)S(1)} %get-tuple-element.5.b_ref), custom_call_target="tpu_custom_call" | custom-call | tf_op jit(solution)/shard_map/pallas_call | solution.py:401
